TPU v7x, 512 devices: a whole 4x8x8 slice. The times are simulated.
512 devices in a mesh: region: 32 (over x, z), tm: 16 (over y, core).
Axes of the slice: x: 4, y: 8, z: 8, core: 2. Of those that a mesh axis runs over, the one named last changes fastest.
Arguments:
- right_side: float32 [1024, 65536], P('tm', 'region'), may hold values from -9 to 9
- initial: float32 [1024, 65536], P('tm', 'region'), may hold values from -1.5 to 1.5
- blocks: bfloat16 [512, 9, 128, 128], P(('region', 'tm')), may hold values from -2.5 to 3.1, as said below
- neighbour_blocks: int32 [512, 8], P('region'), may hold values from 0 to 511, as said below
- temporal_cov: bfloat16 [1024, 1024], P('tm'), may hold values from -2.5 to 2.8, as said below
Outputs:
- solution: float32 [1024, 65536], P('tm', 'region')
- residual: float32 [1024, 65536], P('tm', 'region')
Inputs may be any that keep to these rules, and one draw needn't show every extreme that they name: blocks[i, 0] is symmetric positive definite. `neighbour_blocks`: each column names every block exactly once. Blocks fall into cyclic windows of 16 consecutive blocks starting at 8 + m * 16, and every block listed for row i lies in the window of i. temporal_cov is symmetric positive definite.
All inputs are finite; a program needn't handle non-finite values.
Results may differ from a plain program's by a relative error of at most 0.012.
The roundings to bfloat16 on the way count: a program that leaves them out, or rounds other values in their place, can miss the bound.
Values may be sent and summed in bfloat16 or wider, within the bound.
No kernel may reach another device: no remote copies, remote signals or barrier semaphores. Data moves between devices by JAX's collectives and lax.ppermute only.
A program may use at most 64 MiB of HBM per device.

v0:
```python
import jax
import jax.numpy as jnp
from jax import lax
from jax.sharding import Mesh
from jax.sharding import PartitionSpec as P

ITERS = 2
REGION = ("region_0", "region_1")
TM = ("tm_0", "tm_1")
REGION_TM = ("region_0", "region_1", "tm_0", "tm_1")


def with_halo(value, sides, width):
    for axis, dim in sides:
        peers, length = (lax.axis_size(axis), value.shape[dim])
        up = [(i, (i + 1) % peers) for i in range(peers)]
        down = [(j, i) for i, j in up]
        last = lax.slice_in_dim(value, length - width, length, axis=dim)
        initial = lax.slice_in_dim(value, 0, width, axis=dim)
        before = lax.ppermute(last, axis, up)
        after = lax.ppermute(initial, axis, down)
        value = jnp.concatenate([before, value, after], axis=dim)
    return value


def gather_axes(value, axes, dim):
    for axis in reversed(axes):
        value = lax.all_gather(value, axis, axis=dim, tiled=True)
    return value


def one_axis_at_a_time(value, axes):
    for axis in axes:
        value = lax.psum(value, axis)
    return value


def local_tiles(lowered, neighbour_blocks):
    row_count = neighbour_blocks.shape[0]
    tile_width = lowered.shape[1] // row_count
    widened = with_halo(lowered, ((REGION, 1),), row_count // 2 * tile_width)
    region = lax.axis_index(REGION)
    block_total = row_count * lax.axis_size(REGION)
    offset = jnp.mod(neighbour_blocks - region * row_count + row_count // 2, block_total)
    itself = (jnp.arange(row_count, dtype=jnp.int32) + row_count // 2)[:, None]
    places = jnp.concatenate([itself, offset], axis=1)
    cell_tiles = widened.reshape(widened.shape[0], 2 * row_count, tile_width)
    return jnp.take(cell_tiles, places, axis=1)


def local(right_side, initial, blocks, neighbour_blocks, temporal_cov):
    hour_matrix = gather_axes(temporal_cov, TM, 0)
    region_blocks = lax.all_gather(blocks, TM, axis=0, tiled=True)
    tm_count = lax.axis_size(TM)
    hour_slice = right_side.shape[0]
    site_count = right_side.shape[1]
    tile_width = blocks.shape[2]
    own_rows = blocks.shape[0]

    def temporal(arrived):
        item_count = arrived.shape[2]
        flattened = arrived.reshape(arrived.shape[0], item_count * tile_width)
        blended = jnp.dot(hour_matrix, flattened, preferred_element_type=jnp.float32).astype(
            jnp.bfloat16
        )
        return blended.reshape(arrived.shape[0], 1, item_count, tile_width)

    def operate(current):
        lowered = current.astype(jnp.bfloat16)
        tile_stack = local_tiles(lowered, neighbour_blocks)
        spatial = jnp.einsum(
            "hrkb,rkab->hra", tile_stack, region_blocks, preferred_element_type=jnp.float32
        )
        spatial = spatial.astype(jnp.bfloat16).reshape(hour_slice, tm_count, own_rows, tile_width)
        blended = temporal(lax.all_to_all(spatial, TM, split_axis=1, concat_axis=0, tiled=True))
        returned = lax.all_to_all(blended, TM, split_axis=0, concat_axis=1, tiled=True)
        return current + returned.reshape(hour_slice, site_count).astype(jnp.float32)

    solution = initial
    residual = right_side - operate(initial)
    direction = residual
    norm_now = one_axis_at_a_time(jnp.sum(residual * residual), REGION_TM)
    for iteration in range(ITERS):
        applied = operate(direction)
        curvature, cross_term, square = (
            one_axis_at_a_time(jnp.sum(direction * applied), REGION_TM),
            one_axis_at_a_time(jnp.sum(residual * applied), REGION_TM),
            one_axis_at_a_time(jnp.sum(applied * applied), REGION_TM),
        )
        step_size = norm_now / curvature
        solution = solution + step_size * direction
        norm_next = norm_now - 2.0 * step_size * cross_term + step_size * step_size * square
        residual = residual - step_size * applied
        if iteration + 1 < ITERS:
            direction = residual + norm_next / norm_now * direction
        norm_now = norm_next
    return (solution, residual)


def solution(mesh):
    split = Mesh(mesh.devices.reshape(4, 8, 8, 2), ("region_0", "region_1", "tm_0", "tm_1"))
    return jax.shard_map(
        local,
        mesh=split,
        in_specs=(
            P(TM, REGION),
            P(TM, REGION),
            P(REGION_TM, None, None, None),
            P(REGION, None),
            P(TM, None),
        ),
        out_specs=(P(TM, REGION), P(TM, REGION)),
        check_vma=False,
    )
```

profile of v0, /device:TPU:1, one launch (start us, length us, event | category | flops | bytes accessed | tf_op | source)
XLA Modules:
  0.0 342.4 jit_solution(12038400127978279072)
XLA Ops:
  7.9 10.2 %all_gather.10 = bf16[128,1024]{1,0:T(8,128)(2,1)} all-gather(bf16[64,1024]{1,0:T(8,128)(2,1)} %param.11), channel_id=1, replica_groups=mesh['region_0'=4,'region_1'=8,'tm_0'=8,'tm_1'=2] {'tm_1'}, dimensions={0}, use_global_device_ids=true | all-gather | bytes 393216 | tf_op jit(solution)/shard_map/all_gather | solution.py:28
  21.2 7.5 %collective-permute-start.1 = (bf16[64,1024]{1,0:T(8,128)(2,1)S(1)}, bf16[64,1024]{1,0:T(8,128)(2,1)S(1)}, u32[]{:S(2)}, u32[]{:S(2)}) collective-permute-start(bf16[64,1024]{1,0:T(8,128)(2,1)S(1)} %get-tuple-element.27), channel_id=1, source_target_pairs={{16,0},{32,16},{48,32},{64,48},{80,64},{96,80},{112,96},{128,112},... | collective-permute-start | bytes 393224 | tf_op jit(solution)/shard_map/ppermute | solution.py:21
  32.6 27.8 %all-gather.3.cloned.1.call-done = bf16[16,9,128,128]{3,2,1,0:T(8,128)(2,1)} async-done(((bf16[1,9,128,128]{3,2,1,0:T(8,128)(2,1)}), bf16[16,9,128,128]{3,2,1,0:T(8,128)(2,1)}) %all-gather.3.cloned.1.call-update) | async-done | bytes 4718608 | tf_op jit(solution)/shard_map/all_gather | solution.py:53
  60.5 5.0 %fusion.36 = bf16[64,16,1,128]{3,0,2,1:T(8,128)(2,1)} fusion(bf16[16,9,128,128]{3,2,1,0:T(8,128)(2,1)} %all-gather.3.cloned.1.call-done, bf16[16,9,64,128]{3,2,1,0:T(8,128)(2,1)S(1)} %bitcast.174, pred[16,9]{1,0:T(8,128)(4,1)S(1)} %copy.40), kind=kOutput, calls=%fused_computation.30 | convolution fusion | flops 303300608 | bytes 7340176 | tf_op jit(solution)/shard_map/hrkb,rkab->hra/dot_general | solution.py:71
  65.5 5.0 %all-to-all-start = ((bf16[64,16,1,128]{3,0,2,1:T(8,128)(2,1)}), bf16[64,16,1,128]{3,0,2,1:T(8,128)(2,1)S(1)}, u32[]{:S(2)}, u32[]{:S(2)}) async-start(bf16[64,16,1,128]{3,0,2,1:T(8,128)(2,1)} %fusion.36), calls=%async_computation | async-start | bytes 524288 | tf_op jit(solution)/shard_map/all_to_all | solution.py:75
  70.5 31.9 %all-gather.5.cloned.1.call-done = bf16[1024,1024]{1,0:T(8,128)(2,1)} async-done(((bf16[128,1024]{1,0:T(8,128)(2,1)}), bf16[1024,1024]{1,0:T(8,128)(2,1)}) %all-gather.5.cloned.1.call-update) | async-done | bytes 2097168 | tf_op jit(solution)/shard_map/all_gather | solution.py:28
  106.3 20.0 %all_to_all.72 = bf16[16,2,4096]{2,1,0:T(2,128)(2,1)S(1)} all-to-all(bf16[16,2,4096]{2,1,0:T(2,128)(2,1)S(1)} %reshape.136), channel_id=1, replica_groups=mesh['region_0'=4,'region_1'=8,'tm_0'=8,'tm_1'=2] {'tm_0','tm_1'}, dimensions={0} | all-to-all | bytes 524288 | tf_op jit(solution)/shard_map/all_to_all | solution.py:76
  127.3 3.3 collective-permute-start.2
  130.6 6.4 %collective-permute-start.3 = (bf16[64,1024]{1,0:T(8,128)(2,1)S(1)}, bf16[64,1024]{1,0:T(8,128)(2,1)S(1)}, u32[]{:S(2)}, u32[]{:S(2)}) collective-permute-start(bf16[64,1024]{1,0:T(8,128)(2,1)S(1)} %get-tuple-element.25), channel_id=1, source_target_pairs={{16,0},{32,16},{48,32},{64,48},{80,64},{96,80},{112,96},{128,112},... | collective-permute-start | bytes 393224 | tf_op jit(solution)/shard_map/ppermute | solution.py:21
  142.7 5.1 %fusion.39 = bf16[64,16,1,128]{3,0,2,1:T(8,128)(2,1)S(1)} fusion(bf16[16,9,128,128]{3,2,1,0:T(8,128)(2,1)} %all-gather.3.cloned.1.call-done, bf16[16,9,64,128]{3,2,1,0:T(8,128)(2,1)} %bitcast.176, pred[16,9]{1,0:T(8,128)(4,1)S(1)} %copy.40), kind=kOutput, calls=%fused_computation.31 | convolution fusion | flops 303300608 | bytes 7340176 | tf_op jit(solution)/shard_map/hrkb,rkab->hra/dot_general | solution.py:71
  147.9 14.7 %all_to_all.73 = bf16[64,16,1,128]{3,0,2,1:T(8,128)(2,1)S(1)} all-to-all(bf16[64,16,1,128]{3,0,2,1:T(8,128)(2,1)S(1)} %fusion.39), channel_id=1, replica_groups=mesh['region_0'=4,'region_1'=8,'tm_0'=8,'tm_1'=2] {'tm_0','tm_1'}, dimensions={1} | all-to-all | bytes 524288 | tf_op jit(solution)/shard_map/all_to_all | solution.py:75
  164.5 14.2 %all_to_all.74 = bf16[16,2,4096]{2,1,0:T(2,128)(2,1)S(1)} all-to-all(bf16[16,2,4096]{2,1,0:T(2,128)(2,1)S(1)} %reshape.138), channel_id=1, replica_groups=mesh['region_0'=4,'region_1'=8,'tm_0'=8,'tm_1'=2] {'tm_0','tm_1'}, dimensions={0} | all-to-all | bytes 524288 | tf_op jit(solution)/shard_map/all_to_all | solution.py:76
  180.3 7.2 %all-reduce.2 = (f32[]{:T(128)}, f32[]{:T(128)}, f32[]{:T(128)}) all-reduce(f32[]{:T(128)} %get-tuple-element.5, f32[]{:T(128)} %get-tuple-element.4, f32[]{:T(128)} %get-tuple-element.3), channel_id=1, replica_groups=mesh['region_0'=4,'region_1'=8,'tm_0'=8,'tm_1'=2] {'region_0'}, use_global_device_ids=true, to_apply=%region_1.3 | all-reduce | flops 3 | bytes 24 | tf_op jit(solution)/shard_map/psum | solution.py:34
  187.5 16.8 %all-reduce.1 = (f32[]{:T(128)}, f32[]{:T(128)}, f32[]{:T(128)}) all-reduce(f32[]{:T(128)} %get-tuple-element.12, f32[]{:T(128)} %get-tuple-element.13, f32[]{:T(128)} %get-tuple-element.14), channel_id=1, replica_groups=mesh['region_0'=4,'region_1'=8,'tm_0'=8,'tm_1'=2] {'region_1'}, use_global_device_ids=true, to_apply=%region_2.4 | all-reduce | flops 3 | bytes 24 | tf_op jit(solution)/shard_map/psum | solution.py:34
  204.3 11.7 %all-reduce = (f32[]{:T(128)}, f32[]{:T(128)}, f32[]{:T(128)}) all-reduce(f32[]{:T(128)} %get-tuple-element.9, f32[]{:T(128)} %get-tuple-element.10, f32[]{:T(128)} %get-tuple-element.11), channel_id=1, replica_groups=mesh['region_0'=4,'region_1'=8,'tm_0'=8,'tm_1'=2] {'tm_0'}, use_global_device_ids=true, to_apply=%region_3.5 | all-reduce | flops 3 | bytes 24 | tf_op jit(solution)/shard_map/psum | solution.py:34
  216.0 11.5 %all-reduce.3 = (f32[]{:T(128)}, f32[]{:T(128)}, f32[]{:T(128)}) all-reduce(f32[]{:T(128)} %get-tuple-element.6, f32[]{:T(128)} %get-tuple-element.7, f32[]{:T(128)} %get-tuple-element.8), channel_id=1, replica_groups=mesh['region_0'=4,'region_1'=8,'tm_0'=8,'tm_1'=2] {'tm_1'}, use_global_device_ids=true, to_apply=%region_4.6 | all-reduce | flops 3 | bytes 24 | tf_op jit(solution)/shard_map/psum | solution.py:34
  233.3 6.7 %collective-permute-start.5 = (bf16[64,1024]{1,0:T(8,128)(2,1)S(1)}, bf16[64,1024]{1,0:T(8,128)(2,1)S(1)}, u32[]{:S(2)}, u32[]{:S(2)}) collective-permute-start(bf16[64,1024]{1,0:T(8,128)(2,1)S(1)} %get-tuple-element.23), channel_id=1, source_target_pairs={{16,0},{32,16},{48,32},{64,48},{80,64},{96,80},{112,96},{128,112},... | collective-permute-start | bytes 393224 | tf_op jit(solution)/shard_map/ppermute | solution.py:21
  244.9 5.0 %fusion.42 = bf16[64,16,1,128]{3,0,2,1:T(8,128)(2,1)S(1)} fusion(bf16[16,9,128,128]{3,2,1,0:T(8,128)(2,1)} %all-gather.3.cloned.1.call-done, bf16[16,9,64,128]{3,2,1,0:T(8,128)(2,1)} %bitcast.175, pred[16,9]{1,0:T(8,128)(4,1)S(1)} %copy.40), kind=kOutput, calls=%fused_computation.32 | convolution fusion | flops 303300608 | bytes 7340176 | tf_op jit(solution)/shard_map/hrkb,rkab->hra/dot_general | solution.py:71
  249.9 18.4 %all_to_all.75 = bf16[64,16,1,128]{3,0,2,1:T(8,128)(2,1)S(1)} all-to-all(bf16[64,16,1,128]{3,0,2,1:T(8,128)(2,1)S(1)} %fusion.42), channel_id=1, replica_groups=mesh['region_0'=4,'region_1'=8,'tm_0'=8,'tm_1'=2] {'tm_0','tm_1'}, dimensions={1} | all-to-all | bytes 524288 | tf_op jit(solution)/shard_map/all_to_all | solution.py:75
  270.1 14.5 %all_to_all.76 = bf16[16,2,4096]{2,1,0:T(2,128)(2,1)S(1)} all-to-all(bf16[16,2,4096]{2,1,0:T(2,128)(2,1)S(1)} %reshape.140), channel_id=1, replica_groups=mesh['region_0'=4,'region_1'=8,'tm_0'=8,'tm_1'=2] {'tm_0','tm_1'}, dimensions={0} | all-to-all | bytes 524288 | tf_op jit(solution)/shard_map/all_to_all | solution.py:76
  286.4 6.7 %psum.136 = f32[]{:T(128)} all-reduce(f32[]{:T(128)} %multiply_reduce_fusion), channel_id=1, replica_groups=mesh['region_0'=4,'region_1'=8,'tm_0'=8,'tm_1'=2] {'region_0'}, use_global_device_ids=true, to_apply=%region_16.18 | all-reduce | flops 1 | bytes 8 | tf_op jit(solution)/shard_map/psum | solution.py:34
  293.1 17.2 %psum.137 = f32[]{:T(128)} all-reduce(f32[]{:T(128)} %psum.136), channel_id=1, replica_groups=mesh['region_0'=4,'region_1'=8,'tm_0'=8,'tm_1'=2] {'region_1'}, use_global_device_ids=true, to_apply=%region_17.19 | all-reduce | flops 1 | bytes 8 | tf_op jit(solution)/shard_map/psum | solution.py:34
  310.3 11.6 %psum.138 = f32[]{:T(128)} all-reduce(f32[]{:T(128)} %psum.137), channel_id=1, replica_groups=mesh['region_0'=4,'region_1'=8,'tm_0'=8,'tm_1'=2] {'tm_0'}, use_global_device_ids=true, to_apply=%region_18.20 | all-reduce | flops 1 | bytes 8 | tf_op jit(solution)/shard_map/psum | solution.py:34
  321.9 11.5 %psum.139 = f32[]{:T(128)} all-reduce(f32[]{:T(128)} %psum.138), channel_id=1, replica_groups=mesh['region_0'=4,'region_1'=8,'tm_0'=8,'tm_1'=2] {'tm_1'}, use_global_device_ids=true, to_apply=%region_19.21 | all-reduce | flops 1 | bytes 8 | tf_op jit(solution)/shard_map/psum | solution.py:34
  (73 shorter events, 33.6 us)
Async XLA Ops:
  7.2 53.3 %all-gather.3.cloned.1.call-start = ((), (), s32[]{:S(2)}) async-start(), calls=%async_computation.6 | async-start | bytes 5013504 | tf_op jit(solution)/shard_map/all_gather | solution.py:53
  7.9 94.4 %all-gather.5.cloned.1.call-start = ((), (), s32[]{:S(2)}) async-start(), calls=%async_computation.7 | async-start | bytes 2359296 | tf_op jit(solution)/shard_map/all_gather | solution.py:28
  19.3 11.2 %collective-permute-start = (bf16[64,1024]{1,0:T(8,128)(2,1)S(1)}, bf16[64,1024]{1,0:T(8,128)(2,1)S(1)}, u32[]{:S(2)}, u32[]{:S(2)}) collective-permute-start(bf16[64,1024]{1,0:T(8,128)(2,1)S(1)} %get-tuple-element.26), channel_id=1, source_target_pairs={{0,16},{16,32},{32,48},{48,64},{64,80},{80,96},{96,112},{112,128},... | collective-permute-start | bytes 393224 | tf_op jit(solution)/shard_map/ppermute | solution.py:20
  21.2 10.2 %collective-permute-start.1 = (bf16[64,1024]{1,0:T(8,128)(2,1)S(1)}, bf16[64,1024]{1,0:T(8,128)(2,1)S(1)}, u32[]{:S(2)}, u32[]{:S(2)}) collective-permute-start(bf16[64,1024]{1,0:T(8,128)(2,1)S(1)} %get-tuple-element.27), channel_id=1, source_target_pairs={{16,0},{32,16},{48,32},{64,48},{80,64},{96,80},{112,96},{128,112},... | collective-permute-start | bytes 393224 | tf_op jit(solution)/shard_map/ppermute | solution.py:21
  65.5 36.9 %all-to-all-start = ((bf16[64,16,1,128]{3,0,2,1:T(8,128)(2,1)}), bf16[64,16,1,128]{3,0,2,1:T(8,128)(2,1)S(1)}, u32[]{:S(2)}, u32[]{:S(2)}) async-start(bf16[64,16,1,128]{3,0,2,1:T(8,128)(2,1)} %fusion.36), calls=%async_computation | async-start | bytes 524288 | tf_op jit(solution)/shard_map/all_to_all | solution.py:75
  106.2 20.8 %copy-start.3 = (f32[64,2048]{1,0:T(8,128)S(1)}, f32[64,2048]{1,0:T(8,128)}, u32[]{:S(2)}) copy-start(f32[64,2048]{1,0:T(8,128)} %param.8) | copy-start | bytes 1572868
  106.2 20.8 %copy-start.5 = (f32[64,2048]{1,0:T(8,128)S(1)}, f32[64,2048]{1,0:T(8,128)}, u32[]{:S(2)}) copy-start(f32[64,2048]{1,0:T(8,128)} %param.7) | copy-start | bytes 1572868
  127.3 11.4 %collective-permute-start.2 = (bf16[64,1024]{1,0:T(8,128)(2,1)S(1)}, bf16[64,1024]{1,0:T(8,128)(2,1)S(1)}, u32[]{:S(2)}, u32[]{:S(2)}) collective-permute-start(bf16[64,1024]{1,0:T(8,128)(2,1)S(1)} %get-tuple-element.24), channel_id=1, source_target_pairs={{0,16},{16,32},{32,48},{48,64},{64,80},{80,96},{96,112},{112,128},... | collective-permute-start | bytes 393224 | tf_op jit(solution)/shard_map/ppermute | solution.py:20
  130.6 9.5 %collective-permute-start.3 = (bf16[64,1024]{1,0:T(8,128)(2,1)S(1)}, bf16[64,1024]{1,0:T(8,128)(2,1)S(1)}, u32[]{:S(2)}, u32[]{:S(2)}) collective-permute-start(bf16[64,1024]{1,0:T(8,128)(2,1)S(1)} %get-tuple-element.25), channel_id=1, source_target_pairs={{16,0},{32,16},{48,32},{64,48},{80,64},{96,80},{112,96},{128,112},... | collective-permute-start | bytes 393224 | tf_op jit(solution)/shard_map/ppermute | solution.py:21
  142.7 19.8 %copy-start = (bf16[1024,1024]{1,0:T(8,128)(2,1)S(1)}, bf16[1024,1024]{1,0:T(8,128)(2,1)}, u32[]{:S(2)}) copy-start(bf16[1024,1024]{1,0:T(8,128)(2,1)} %all-gather.5.cloned.1.call-done) | copy-start | bytes 6291460
  179.4 62.0 %copy-start.1 = (f32[64,16,1,1,128]{4,1,0,3,2:T(8,128)}, f32[64,16,1,1,128]{4,1,0,3,2:T(8,128)S(1)}, u32[]{:S(2)}) copy-start(f32[64,16,1,1,128]{4,1,0,3,2:T(8,128)S(1)} %copy.53) | copy-start | bytes 1572868
  231.4 9.9 %collective-permute-start.4 = (bf16[64,1024]{1,0:T(8,128)(2,1)S(1)}, bf16[64,1024]{1,0:T(8,128)(2,1)S(1)}, u32[]{:S(2)}, u32[]{:S(2)}) collective-permute-start(bf16[64,1024]{1,0:T(8,128)(2,1)S(1)} %get-tuple-element.22), channel_id=1, source_target_pairs={{0,16},{16,32},{32,48},{48,64},{64,80},{80,96},{96,112},{112,128},... | collective-permute-start | bytes 393224 | tf_op jit(solution)/shard_map/ppermute | solution.py:20
  233.3 8.9 %collective-permute-start.5 = (bf16[64,1024]{1,0:T(8,128)(2,1)S(1)}, bf16[64,1024]{1,0:T(8,128)(2,1)S(1)}, u32[]{:S(2)}, u32[]{:S(2)}) collective-permute-start(bf16[64,1024]{1,0:T(8,128)(2,1)S(1)} %get-tuple-element.23), channel_id=1, source_target_pairs={{16,0},{32,16},{48,32},{64,48},{80,64},{96,80},{112,96},{128,112},... | collective-permute-start | bytes 393224 | tf_op jit(solution)/shard_map/ppermute | solution.py:21
  270.1 15.3 %copy-start.2 = (f32[64,16,1,1,128]{4,1,0,3,2:T(8,128)S(1)}, f32[64,16,1,1,128]{4,1,0,3,2:T(8,128)}, u32[]{:S(2)}) copy-start(f32[64,16,1,1,128]{4,1,0,3,2:T(8,128)} %copy-done.1) | copy-start | bytes 1572868
  284.6 49.4 %copy-start.4 = (f32[64,2048]{1,0:T(8,128)S(1)}, f32[64,2048]{1,0:T(8,128)}, u32[]{:S(2)}) copy-start(f32[64,2048]{1,0:T(8,128)} %param.8) | copy-start | bytes 1572868
Sparse Core Ops, SparseCore 0:
  10.1 50.3 all-gather.2
  62.5 39.7 all-gather.4
where the time goes:
time: 343 us; the launch traced here: 342 us
  blocking collectives  186 us (54%)
  waiting for transfers between devices  67.4 us (20%)
  starting transfers between devices  32.7 us (10%)
  matrix products  19.2 us (6%)
  between operations  18.8 us (5%)
  local copies, waits for them, and re-layouts  9.38 us (3%)
  other arithmetic  8.5 us (2%)
    psum x8, blocking collectives, one_axis_at_a_time(): value = lax.psum(value, axis)  94.3 us
    all_to_all x3, blocking collectives, operate(): lax.all_to_all(blended, TM, split_axis=0, concat_axis=1, tiled=True)  48.7 us
    all_to_all x2, blocking collectives, operate(): lax.all_to_all(spatial, TM, split_axis=1, concat_axis=0, tiled=True)  33.1 us
    all_gather x1, waiting for transfers between devices, gather_axes(): value = lax.all_gather(value, axis, axis=dim, tiled=True)  31.9 us
    all_gather x1, waiting for transfers between devices, local(): region_blocks = lax.all_gather(blocks, TM, axis=0, tiled=True)  27.8 us
    ppermute x3, starting transfers between devices, with_halo(): after = lax.ppermute(initial, axis, down)  20.6 us
    dot_general x3, matrix products, operate(): jnp.einsum('hrkb,rkab->hra', tile_stack, region_blocks, preferred_element...  15.1 us
    all_gather x1, blocking collectives, gather_axes(): value = lax.all_gather(value, axis, axis=dim, tiled=True)  10.2 us
  transfers between devices with their start and end apart: 9, of which 8 were waited for; matrix products, arithmetic and copies ran while one was open for 2% of the time, Pallas kernels for 0%

commit v1 on v0

--- a/solution.py
+++ b/solution.py
@@ -73,7 +73,9 @@
         )
         spatial = spatial.astype(jnp.bfloat16).reshape(hour_slice, tm_count, own_rows, tile_width)
         blended = temporal(lax.all_to_all(spatial, TM, split_axis=1, concat_axis=0, tiled=True))
-        returned = lax.all_to_all(blended, TM, split_axis=0, concat_axis=1, tiled=True)
+        pieces = jnp.split(blended, lax.axis_size(TM), axis=0)
+        arrived_2 = lax.all_to_all(jnp.stack(pieces), TM, 0, 0)
+        returned = jnp.concatenate(arrived_2, axis=1)
         return current + returned.reshape(hour_slice, site_count).astype(jnp.float32)
 
     solution = initial

time: 343 us -> 342 us (level)
  no operation moved by 1% of the time
where the time goes in v1:
time: 342 us; the launch traced here: 341 us
  blocking collectives  186 us (54%)
  waiting for transfers between devices  67.4 us (20%)
  starting transfers between devices  32.7 us (10%)
  matrix products  19.2 us (6%)
  between operations  19.1 us (6%)
  local copies, waits for them, and re-layouts  10.7 us (3%)
  other arithmetic  6.13 us (2%)
    psum x8, blocking collectives, one_axis_at_a_time(): value = lax.psum(value, axis)  94.3 us
    all_to_all x3, blocking collectives, operate(): arrived_2 = lax.all_to_all(jnp.stack(pieces), TM, 0, 0)  48.5 us
    all_to_all x2, blocking collectives, operate(): lax.all_to_all(spatial, TM, split_axis=1, concat_axis=0, tiled=True)  33.1 us
    all_gather x1, waiting for transfers between devices, gather_axes(): value = lax.all_gather(value, axis, axis=dim, tiled=True)  31.9 us
    all_gather x1, waiting for transfers between devices, local(): region_blocks = lax.all_gather(blocks, TM, axis=0, tiled=True)  27.8 us
    ppermute x3, starting transfers between devices, with_halo(): after = lax.ppermute(initial, axis, down)  20.6 us
    dot_general x3, matrix products, operate(): jnp.einsum('hrkb,rkab->hra', tile_stack, region_blocks, preferred_element...  15.1 us
    all_gather x1, blocking collectives, gather_axes(): value = lax.all_gather(value, axis, axis=dim, tiled=True)  10.2 us
  transfers between devices with their start and end apart: 9, of which 8 were waited for; matrix products, arithmetic and copies ran while one was open for 2% of the time, Pallas kernels for 0%

profile of v1, /device:TPU:1, one launch (start us, length us, event | category | flops | bytes accessed | tf_op | source)
XLA Modules:
  0.0 341.4 jit_solution(2667462321026639514)
XLA Ops:
  7.9 10.2 %all_gather.10 = bf16[128,1024]{1,0:T(8,128)(2,1)} all-gather(bf16[64,1024]{1,0:T(8,128)(2,1)} %param.11), channel_id=1, replica_groups=mesh['region_0'=4,'region_1'=8,'tm_0'=8,'tm_1'=2] {'tm_1'}, dimensions={0}, use_global_device_ids=true | all-gather | bytes 393216 | tf_op jit(solution)/shard_map/all_gather | solution.py:28
  21.2 7.5 %collective-permute-start.1 = (bf16[64,1024]{1,0:T(8,128)(2,1)S(1)}, bf16[64,1024]{1,0:T(8,128)(2,1)S(1)}, u32[]{:S(2)}, u32[]{:S(2)}) collective-permute-start(bf16[64,1024]{1,0:T(8,128)(2,1)S(1)} %get-tuple-element.27), channel_id=1, source_target_pairs={{16,0},{32,16},{48,32},{64,48},{80,64},{96,80},{112,96},{128,112},... | collective-permute-start | bytes 393224 | tf_op jit(solution)/shard_map/ppermute | solution.py:21
  32.6 27.8 %all-gather.3.cloned.1.call-done = bf16[16,9,128,128]{3,2,1,0:T(8,128)(2,1)} async-done(((bf16[1,9,128,128]{3,2,1,0:T(8,128)(2,1)}), bf16[16,9,128,128]{3,2,1,0:T(8,128)(2,1)}) %all-gather.3.cloned.1.call-update) | async-done | bytes 4718608 | tf_op jit(solution)/shard_map/all_gather | solution.py:53
  60.5 5.0 %fusion.36 = bf16[64,16,1,128]{3,0,2,1:T(8,128)(2,1)} fusion(bf16[16,9,128,128]{3,2,1,0:T(8,128)(2,1)} %all-gather.3.cloned.1.call-done, bf16[16,9,64,128]{3,2,1,0:T(8,128)(2,1)S(1)} %bitcast.354, pred[16,9]{1,0:T(8,128)(4,1)S(1)} %copy.52), kind=kOutput, calls=%fused_computation.30 | convolution fusion | flops 303300608 | bytes 7340176 | tf_op jit(solution)/shard_map/hrkb,rkab->hra/dot_general | solution.py:71
  65.5 5.0 %all-to-all-start = ((bf16[64,16,1,128]{3,0,2,1:T(8,128)(2,1)}), bf16[64,16,1,128]{3,0,2,1:T(8,128)(2,1)S(1)}, u32[]{:S(2)}, u32[]{:S(2)}) async-start(bf16[64,16,1,128]{3,0,2,1:T(8,128)(2,1)} %fusion.36), calls=%async_computation | async-start | bytes 524288 | tf_op jit(solution)/shard_map/all_to_all | solution.py:75
  70.5 31.9 %all-gather.5.cloned.1.call-done = bf16[1024,1024]{1,0:T(8,128)(2,1)} async-done(((bf16[128,1024]{1,0:T(8,128)(2,1)}), bf16[1024,1024]{1,0:T(8,128)(2,1)}) %all-gather.5.cloned.1.call-update) | async-done | bytes 2097168 | tf_op jit(solution)/shard_map/all_gather | solution.py:28
  106.0 19.9 %all_to_all.60 = bf16[16,64,1,1,128]{4,1,3,2,0:T(8,128)(2,1)S(1)} all-to-all(bf16[16,64,1,1,128]{4,1,3,2,0:T(8,128)(2,1)S(1)} %copy.56), channel_id=1, replica_groups=mesh['region_0'=4,'region_1'=8,'tm_0'=8,'tm_1'=2] {'tm_0','tm_1'}, dimensions={0} | all-to-all | bytes 524288 | tf_op jit(solution)/shard_map/all_to_all | solution.py:77
  126.5 3.3 collective-permute-start.2
  129.8 6.4 %collective-permute-start.3 = (bf16[64,1024]{1,0:T(8,128)(2,1)S(1)}, bf16[64,1024]{1,0:T(8,128)(2,1)S(1)}, u32[]{:S(2)}, u32[]{:S(2)}) collective-permute-start(bf16[64,1024]{1,0:T(8,128)(2,1)S(1)} %get-tuple-element.25), channel_id=1, source_target_pairs={{16,0},{32,16},{48,32},{64,48},{80,64},{96,80},{112,96},{128,112},... | collective-permute-start | bytes 393224 | tf_op jit(solution)/shard_map/ppermute | solution.py:21
  142.0 5.1 %fusion.39 = bf16[64,16,1,128]{3,0,2,1:T(8,128)(2,1)S(1)} fusion(bf16[16,9,128,128]{3,2,1,0:T(8,128)(2,1)} %all-gather.3.cloned.1.call-done, bf16[16,9,64,128]{3,2,1,0:T(8,128)(2,1)} %bitcast.356, pred[16,9]{1,0:T(8,128)(4,1)S(1)} %copy.52), kind=kOutput, calls=%fused_computation.31 | convolution fusion | flops 303300608 | bytes 7340176 | tf_op jit(solution)/shard_map/hrkb,rkab->hra/dot_general | solution.py:71
  147.1 14.7 %all_to_all.61 = bf16[64,16,1,128]{3,0,2,1:T(8,128)(2,1)S(1)} all-to-all(bf16[64,16,1,128]{3,0,2,1:T(8,128)(2,1)S(1)} %fusion.39), channel_id=1, replica_groups=mesh['region_0'=4,'region_1'=8,'tm_0'=8,'tm_1'=2] {'tm_0','tm_1'}, dimensions={1} | all-to-all | bytes 524288 | tf_op jit(solution)/shard_map/all_to_all | solution.py:75
  163.8 14.2 %all_to_all.62 = bf16[16,64,1,1,128]{4,1,3,2,0:T(8,128)(2,1)S(1)} all-to-all(bf16[16,64,1,1,128]{4,1,3,2,0:T(8,128)(2,1)S(1)} %copy.62), channel_id=1, replica_groups=mesh['region_0'=4,'region_1'=8,'tm_0'=8,'tm_1'=2] {'tm_0','tm_1'}, dimensions={0} | all-to-all | bytes 524288 | tf_op jit(solution)/shard_map/all_to_all | solution.py:77
  179.3 7.2 %all-reduce.2 = (f32[]{:T(128)}, f32[]{:T(128)}, f32[]{:T(128)}) all-reduce(f32[]{:T(128)} %get-tuple-element.5, f32[]{:T(128)} %get-tuple-element.4, f32[]{:T(128)} %get-tuple-element.3), channel_id=1, replica_groups=mesh['region_0'=4,'region_1'=8,'tm_0'=8,'tm_1'=2] {'region_0'}, use_global_device_ids=true, to_apply=%region_1.3 | all-reduce | flops 3 | bytes 24 | tf_op jit(solution)/shard_map/psum | solution.py:34
  186.6 16.8 %all-reduce.1 = (f32[]{:T(128)}, f32[]{:T(128)}, f32[]{:T(128)}) all-reduce(f32[]{:T(128)} %get-tuple-element.12, f32[]{:T(128)} %get-tuple-element.13, f32[]{:T(128)} %get-tuple-element.14), channel_id=1, replica_groups=mesh['region_0'=4,'region_1'=8,'tm_0'=8,'tm_1'=2] {'region_1'}, use_global_device_ids=true, to_apply=%region_2.4 | all-reduce | flops 3 | bytes 24 | tf_op jit(solution)/shard_map/psum | solution.py:34
  203.4 11.7 %all-reduce = (f32[]{:T(128)}, f32[]{:T(128)}, f32[]{:T(128)}) all-reduce(f32[]{:T(128)} %get-tuple-element.9, f32[]{:T(128)} %get-tuple-element.10, f32[]{:T(128)} %get-tuple-element.11), channel_id=1, replica_groups=mesh['region_0'=4,'region_1'=8,'tm_0'=8,'tm_1'=2] {'tm_0'}, use_global_device_ids=true, to_apply=%region_3.5 | all-reduce | flops 3 | bytes 24 | tf_op jit(solution)/shard_map/psum | solution.py:34
  215.1 11.5 %all-reduce.3 = (f32[]{:T(128)}, f32[]{:T(128)}, f32[]{:T(128)}) all-reduce(f32[]{:T(128)} %get-tuple-element.6, f32[]{:T(128)} %get-tuple-element.7, f32[]{:T(128)} %get-tuple-element.8), channel_id=1, replica_groups=mesh['region_0'=4,'region_1'=8,'tm_0'=8,'tm_1'=2] {'tm_1'}, use_global_device_ids=true, to_apply=%region_4.6 | all-reduce | flops 3 | bytes 24 | tf_op jit(solution)/shard_map/psum | solution.py:34
  232.6 6.7 %collective-permute-start.5 = (bf16[64,1024]{1,0:T(8,128)(2,1)S(1)}, bf16[64,1024]{1,0:T(8,128)(2,1)S(1)}, u32[]{:S(2)}, u32[]{:S(2)}) collective-permute-start(bf16[64,1024]{1,0:T(8,128)(2,1)S(1)} %get-tuple-element.23), channel_id=1, source_target_pairs={{16,0},{32,16},{48,32},{64,48},{80,64},{96,80},{112,96},{128,112},... | collective-permute-start | bytes 393224 | tf_op jit(solution)/shard_map/ppermute | solution.py:21
  244.2 5.0 %fusion.42 = bf16[64,16,1,128]{3,0,2,1:T(8,128)(2,1)S(1)} fusion(bf16[16,9,128,128]{3,2,1,0:T(8,128)(2,1)} %all-gather.3.cloned.1.call-done, bf16[16,9,64,128]{3,2,1,0:T(8,128)(2,1)} %bitcast.355, pred[16,9]{1,0:T(8,128)(4,1)S(1)} %copy.52), kind=kOutput, calls=%fused_computation.32 | convolution fusion | flops 303300608 | bytes 7340176 | tf_op jit(solution)/shard_map/hrkb,rkab->hra/dot_general | solution.py:71
  249.2 18.4 %all_to_all.63 = bf16[64,16,1,128]{3,0,2,1:T(8,128)(2,1)S(1)} all-to-all(bf16[64,16,1,128]{3,0,2,1:T(8,128)(2,1)S(1)} %fusion.42), channel_id=1, replica_groups=mesh['region_0'=4,'region_1'=8,'tm_0'=8,'tm_1'=2] {'tm_0','tm_1'}, dimensions={1} | all-to-all | bytes 524288 | tf_op jit(solution)/shard_map/all_to_all | solution.py:75
  269.6 14.4 %all_to_all.64 = bf16[16,64,1,1,128]{4,1,3,2,0:T(8,128)(2,1)S(1)} all-to-all(bf16[16,64,1,1,128]{4,1,3,2,0:T(8,128)(2,1)S(1)} %copy.68), channel_id=1, replica_groups=mesh['region_0'=4,'region_1'=8,'tm_0'=8,'tm_1'=2] {'tm_0','tm_1'}, dimensions={0} | all-to-all | bytes 524288 | tf_op jit(solution)/shard_map/all_to_all | solution.py:77
  285.4 6.7 %psum.136 = f32[]{:T(128)} all-reduce(f32[]{:T(128)} %multiply_reduce_fusion), channel_id=1, replica_groups=mesh['region_0'=4,'region_1'=8,'tm_0'=8,'tm_1'=2] {'region_0'}, use_global_device_ids=true, to_apply=%region_16.18 | all-reduce | flops 1 | bytes 8 | tf_op jit(solution)/shard_map/psum | solution.py:34
  292.1 17.2 %psum.137 = f32[]{:T(128)} all-reduce(f32[]{:T(128)} %psum.136), channel_id=1, replica_groups=mesh['region_0'=4,'region_1'=8,'tm_0'=8,'tm_1'=2] {'region_1'}, use_global_device_ids=true, to_apply=%region_17.19 | all-reduce | flops 1 | bytes 8 | tf_op jit(solution)/shard_map/psum | solution.py:34
  309.3 11.6 %psum.138 = f32[]{:T(128)} all-reduce(f32[]{:T(128)} %psum.137), channel_id=1, replica_groups=mesh['region_0'=4,'region_1'=8,'tm_0'=8,'tm_1'=2] {'tm_0'}, use_global_device_ids=true, to_apply=%region_18.20 | all-reduce | flops 1 | bytes 8 | tf_op jit(solution)/shard_map/psum | solution.py:34
  320.9 11.5 %psum.139 = f32[]{:T(128)} all-reduce(f32[]{:T(128)} %psum.138), channel_id=1, replica_groups=mesh['region_0'=4,'region_1'=8,'tm_0'=8,'tm_1'=2] {'tm_1'}, use_global_device_ids=true, to_apply=%region_19.21 | all-reduce | flops 1 | bytes 8 | tf_op jit(solution)/shard_map/psum | solution.py:34
  (108 shorter events, 32.6 us)
Async XLA Ops:
  7.2 53.3 %all-gather.3.cloned.1.call-start = ((), (), s32[]{:S(2)}) async-start(), calls=%async_computation.6 | async-start | bytes 5013504 | tf_op jit(solution)/shard_map/all_gather | solution.py:53
  7.9 94.4 %all-gather.5.cloned.1.call-start = ((), (), s32[]{:S(2)}) async-start(), calls=%async_computation.7 | async-start | bytes 2359296 | tf_op jit(solution)/shard_map/all_gather | solution.py:28
  19.3 11.2 %collective-permute-start = (bf16[64,1024]{1,0:T(8,128)(2,1)S(1)}, bf16[64,1024]{1,0:T(8,128)(2,1)S(1)}, u32[]{:S(2)}, u32[]{:S(2)}) collective-permute-start(bf16[64,1024]{1,0:T(8,128)(2,1)S(1)} %get-tuple-element.26), channel_id=1, source_target_pairs={{0,16},{16,32},{32,48},{48,64},{64,80},{80,96},{96,112},{112,128},... | collective-permute-start | bytes 393224 | tf_op jit(solution)/shard_map/ppermute | solution.py:20
  21.2 10.2 %collective-permute-start.1 = (bf16[64,1024]{1,0:T(8,128)(2,1)S(1)}, bf16[64,1024]{1,0:T(8,128)(2,1)S(1)}, u32[]{:S(2)}, u32[]{:S(2)}) collective-permute-start(bf16[64,1024]{1,0:T(8,128)(2,1)S(1)} %get-tuple-element.27), channel_id=1, source_target_pairs={{16,0},{32,16},{48,32},{64,48},{80,64},{96,80},{112,96},{128,112},... | collective-permute-start | bytes 393224 | tf_op jit(solution)/shard_map/ppermute | solution.py:21
  65.5 36.9 %all-to-all-start = ((bf16[64,16,1,128]{3,0,2,1:T(8,128)(2,1)}), bf16[64,16,1,128]{3,0,2,1:T(8,128)(2,1)S(1)}, u32[]{:S(2)}, u32[]{:S(2)}) async-start(bf16[64,16,1,128]{3,0,2,1:T(8,128)(2,1)} %fusion.36), calls=%async_computation | async-start | bytes 524288 | tf_op jit(solution)/shard_map/all_to_all | solution.py:75
  104.7 21.5 %copy-start.3 = (f32[64,2048]{1,0:T(8,128)S(1)}, f32[64,2048]{1,0:T(8,128)}, u32[]{:S(2)}) copy-start(f32[64,2048]{1,0:T(8,128)} %param.8) | copy-start | bytes 1572868
  104.8 21.5 %copy-start.5 = (f32[64,2048]{1,0:T(8,128)S(1)}, f32[64,2048]{1,0:T(8,128)}, u32[]{:S(2)}) copy-start(f32[64,2048]{1,0:T(8,128)} %param.7) | copy-start | bytes 1572868
  126.5 11.4 %collective-permute-start.2 = (bf16[64,1024]{1,0:T(8,128)(2,1)S(1)}, bf16[64,1024]{1,0:T(8,128)(2,1)S(1)}, u32[]{:S(2)}, u32[]{:S(2)}) collective-permute-start(bf16[64,1024]{1,0:T(8,128)(2,1)S(1)} %get-tuple-element.24), channel_id=1, source_target_pairs={{0,16},{16,32},{32,48},{48,64},{64,80},{80,96},{96,112},{112,128},... | collective-permute-start | bytes 393224 | tf_op jit(solution)/shard_map/ppermute | solution.py:20
  129.8 9.5 %collective-permute-start.3 = (bf16[64,1024]{1,0:T(8,128)(2,1)S(1)}, bf16[64,1024]{1,0:T(8,128)(2,1)S(1)}, u32[]{:S(2)}, u32[]{:S(2)}) collective-permute-start(bf16[64,1024]{1,0:T(8,128)(2,1)S(1)} %get-tuple-element.25), channel_id=1, source_target_pairs={{16,0},{32,16},{48,32},{64,48},{80,64},{96,80},{112,96},{128,112},... | collective-permute-start | bytes 393224 | tf_op jit(solution)/shard_map/ppermute | solution.py:21
  142.0 19.8 %copy-start = (bf16[1024,1024]{1,0:T(8,128)(2,1)S(1)}, bf16[1024,1024]{1,0:T(8,128)(2,1)}, u32[]{:S(2)}) copy-start(bf16[1024,1024]{1,0:T(8,128)(2,1)} %all-gather.5.cloned.1.call-done) | copy-start | bytes 6291460
  178.4 62.2 %copy-start.1 = (f32[64,16,1,1,128]{4,1,0,3,2:T(8,128)}, f32[64,16,1,1,128]{4,1,0,3,2:T(8,128)S(1)}, u32[]{:S(2)}) copy-start(f32[64,16,1,1,128]{4,1,0,3,2:T(8,128)S(1)} %copy.63) | copy-start | bytes 1572868
  230.7 9.9 %collective-permute-start.4 = (bf16[64,1024]{1,0:T(8,128)(2,1)S(1)}, bf16[64,1024]{1,0:T(8,128)(2,1)S(1)}, u32[]{:S(2)}, u32[]{:S(2)}) collective-permute-start(bf16[64,1024]{1,0:T(8,128)(2,1)S(1)} %get-tuple-element.22), channel_id=1, source_target_pairs={{0,16},{16,32},{32,48},{48,64},{64,80},{80,96},{96,112},{112,128},... | collective-permute-start | bytes 393224 | tf_op jit(solution)/shard_map/ppermute | solution.py:20
  232.6 8.9 %collective-permute-start.5 = (bf16[64,1024]{1,0:T(8,128)(2,1)S(1)}, bf16[64,1024]{1,0:T(8,128)(2,1)S(1)}, u32[]{:S(2)}, u32[]{:S(2)}) collective-permute-start(bf16[64,1024]{1,0:T(8,128)(2,1)S(1)} %get-tuple-element.23), channel_id=1, source_target_pairs={{16,0},{32,16},{48,32},{64,48},{80,64},{96,80},{112,96},{128,112},... | collective-permute-start | bytes 393224 | tf_op jit(solution)/shard_map/ppermute | solution.py:21
  268.4 16.0 %copy-start.2 = (f32[64,16,1,1,128]{4,1,0,3,2:T(8,128)S(1)}, f32[64,16,1,1,128]{4,1,0,3,2:T(8,128)}, u32[]{:S(2)}) copy-start(f32[64,16,1,1,128]{4,1,0,3,2:T(8,128)} %copy-done.1) | copy-start | bytes 1572868
  269.4 63.7 %copy-start.4 = (f32[64,2048]{1,0:T(8,128)S(1)}, f32[64,2048]{1,0:T(8,128)}, u32[]{:S(2)}) copy-start(f32[64,2048]{1,0:T(8,128)} %param.8) | copy-start | bytes 1572868
Sparse Core Ops, SparseCore 0:
  10.1 50.3 all-gather.2
  62.5 39.7 all-gather.4
